TPU v7x, 32 devices: a whole 2x2x4 slice. The times are simulated.
32 devices in a mesh: rcv: 4 (over y, core), slab: 8 (over z, x).
Axes of the slice: x: 2, y: 2, z: 4, core: 2. Of those that a mesh axis runs over, the one named last changes fastest.
Arguments:
- displacement: bfloat16 [2, 16, 3, 16, 16, 1024], P(None, None, None, 'slab'), may hold values from -6 to 6
- green: bfloat16 [8, 16, 6, 16, 16, 1024], P('rcv', None, None, 'slab'), may hold values from -0.1796875 to 0.1796875
- lame_lambda: float32 [16, 16, 1024], P('slab'), may hold values from 0.5 to 2
- shear_modulus: float32 [16, 16, 1024], P('slab'), may hold values from 0.3 to 1.5
- filters: float32 [2, 8, 9], P(None, 'rcv'), may hold values from -2 to 2
- pairs: int32 [2, 8], P(None, 'rcv'), may hold values 0 or 1
Outputs:
- kernels: float32 [2, 16, 16, 1024], P(None, 'slab', 'rcv')
Inputs may be any that keep to these rules, and one draw needn't show every extreme that they name: `pairs`: 1 marks a pair that is used, 0 one that is not.
All inputs are finite; a program needn't handle non-finite values. No bound on the sum of `pairs` on one device may be relied on, other than what follows from the above.
Results may differ from a plain program's by a relative error of at most 0.0029.
Values may be sent and summed in bfloat16 or wider, within the bound.
No kernel may reach another device: no remote copies, remote signals or barrier semaphores. Data moves between devices by JAX's collectives and lax.ppermute only.
A program may use at most 192 MiB of HBM per device.

v0:
```python
import jax
import jax.numpy as jnp
from jax import lax
from jax.sharding import PartitionSpec as P


def padded_2(array, sides, width):
    for axis, dim in sides:
        devices, length = (lax.axis_size(axis), array.shape[dim])
        up = [(i, (i + 1) % devices) for i in range(devices - 1)]
        down = [(j, i) for i, j in up]
        last = lax.slice_in_dim(array, length - width, length, axis=dim)
        initial = lax.slice_in_dim(array, 0, width, axis=dim)
        before = lax.ppermute(last, axis, up)
        after = lax.ppermute(initial, axis, down)
        array = jnp.concatenate([before, array, after], axis=dim)
    return array


def derivative(field, axis):
    length = field.shape[axis]
    pad_width = [(0, 0)] * field.ndim
    pad_width[axis] = (2, 2)
    padded = jnp.pad(field, pad_width)

    def window(offset):
        return lax.slice_in_dim(padded, 2 + offset, 2 + offset + length, axis=axis)

    return (8.0 * (window(1) - window(-1)) - (window(2) - window(-2))) / 12.0


def depth_derivative(extended, length):

    def window(offset):
        return lax.slice_in_dim(extended, 2 + offset, 2 + offset + length, axis=3)

    return (8.0 * (window(1) - window(-1)) - (window(2) - window(-2))) / 12.0


def compose(along_cols, along_rows, along_depth, lame_lambda, shear_modulus):
    strain_xx = along_cols[:, :, 0]
    strain_yy = along_rows[:, :, 1]
    strain_zz = along_depth[:, :, 2]
    strain_yz = 0.5 * (along_depth[:, :, 1] + along_rows[:, :, 2])
    strain_xz = 0.5 * (along_depth[:, :, 0] + along_cols[:, :, 2])
    strain_xy = 0.5 * (along_rows[:, :, 0] + along_cols[:, :, 1])
    strain_trace = strain_xx + strain_yy + strain_zz
    volume_term = lame_lambda * strain_trace
    double_shear = 2.0 * shear_modulus
    components = [
        volume_term + double_shear * strain_xx,
        volume_term + double_shear * strain_yy,
        volume_term + double_shear * strain_zz,
        double_shear * strain_yz,
        double_shear * strain_xz,
        double_shear * strain_xy,
    ]
    return jnp.stack(components, axis=2).astype(jnp.bfloat16)


def contribution(stress_one, filter_taps, green_one):
    lag_total = filter_taps.shape[0]
    half_lags = lag_total // 2
    snap_count = stress_one.shape[0]
    padded = jnp.pad(stress_one, [(half_lags, half_lags)] + [(0, 0)] * (stress_one.ndim - 1))
    filtered = jnp.zeros(stress_one.shape, jnp.float32)
    for lag_index in range(lag_total):
        filtered = filtered + filter_taps[lag_index] * padded[
            lag_index : lag_index + snap_count
        ].astype(jnp.float32)
    weights = jnp.array([1.0, 1.0, 1.0, 2.0, 2.0, 2.0], jnp.float32).reshape(1, 6, 1, 1, 1)
    return jnp.sum(filtered * green_one.astype(jnp.float32) * weights, axis=(0, 1))


def on_device(displacement, green, lame_lambda, shear_modulus, filters, pairs):
    sources, snap_count, components, planes, row_count, col_count = displacement.shape
    groups = lax.axis_size("rcv")
    member = lax.axis_index("rcv")
    flat = displacement.reshape((sources * snap_count, components, planes, row_count, col_count))
    share = flat.shape[0] // groups
    mine = lax.dynamic_slice_in_dim(flat, member * share, share, 0)
    grown = padded_2(mine, (("slab", 2),), 2)
    edges = jnp.concatenate([grown[:, :, 0:2], grown[:, :, planes + 2 : planes + 4]], axis=2)
    every_edge = lax.all_gather(edges, "rcv", axis=0, tiled=True)
    joined = jnp.concatenate([every_edge[:, :, 0:2], flat, every_edge[:, :, 2:4]], axis=2)
    extended = joined.reshape((sources, snap_count, components, planes + 4, row_count, col_count))
    field = extended.astype(jnp.float32)
    interior = field[:, :, :, 2 : planes + 2]
    along_depth = depth_derivative(field, planes)
    along_rows = derivative(interior, 4)
    along_cols = derivative(interior, 5)
    stress = compose(along_cols, along_rows, along_depth, lame_lambda, shear_modulus)
    station_count = green.shape[0]
    slots = sources * station_count
    flat_pairs = pairs.reshape(-1)
    initial = jnp.zeros((sources, planes, row_count, col_count), jnp.float32)

    def add_slot(slot, kernel_acc, weight):
        source = slot // station_count
        station = slot % station_count
        stress_one = lax.dynamic_index_in_dim(stress, source, 0, keepdims=False)
        green_one = lax.dynamic_index_in_dim(green, station, 0, keepdims=False)
        filter_taps = filters[source, station]
        term = weight * contribution(stress_one, filter_taps, green_one)
        current = lax.dynamic_index_in_dim(kernel_acc, source, 0, keepdims=False)
        return lax.dynamic_update_index_in_dim(kernel_acc, current + term, source, 0)

    def add_masked(slot, kernel_acc):
        return add_slot(slot, kernel_acc, flat_pairs[slot].astype(jnp.float32))

    kernel_acc = lax.fori_loop(0, slots, add_masked, initial)
    return lax.psum_scatter(kernel_acc, "rcv", scatter_dimension=2, tiled=True)


def solution(mesh):
    placed = (
        P(None, None, None, "slab", None, None),
        P("rcv", None, None, "slab", None, None),
        P("slab", None, None),
        P("slab", None, None),
        P(None, "rcv", None),
        P(None, "rcv"),
    )
    return jax.shard_map(
        on_device,
        mesh=mesh,
        in_specs=placed,
        out_specs=P(None, "slab", "rcv", None),
        check_vma=False,
    )
```

profile of v0, /device:TPU:0, one launch (start us, length us, event | category | flops | bytes accessed | tf_op | source)
XLA Modules:
  0.0 495.1 jit_solution(11546847999297486046)
XLA Ops:
  6.5 0.0 copy-start.5
  6.5 0.0 copy-start.2
  6.5 0.0 all-gather.2.cloned.1.call-start
  6.5 1.6 constant_dynamic-slice_fusion.2
  8.2 5.0 %collective-permute-start = (bf16[8,3,2,16,1024]{4,3,2,1,0:T(8,128)(2,1)S(1)}, bf16[8,3,2,16,1024]{4,3,2,1,0:T(8,128)(2,1)S(1)}, u32[]{:S(2)}, u32[]{:S(2)}) collective-permute-start(bf16[8,3,2,16,1024]{4,3,2,1,0:T(8,128)(2,1)S(1)} %constant_dynamic-slice_fusion.2), channel_id=1, source_target_pairs={{0,1},{1,2},{2,3},{3,4},{4,5},{5,6},{6,7},{8,9},{9,10},{10,11},{11... | collective-permute-start | bytes 4718600 | tf_op jit(solution)/shard_map/ppermute | solution.py:14
  13.1 1.3 collective-permute-start.1
  14.4 65.9 %collective-permute-done = bf16[8,3,2,16,1024]{4,3,2,1,0:T(8,128)(2,1)S(1)} collective-permute-done((bf16[8,3,2,16,1024]{4,3,2,1,0:T(8,128)(2,1)S(1)}, bf16[8,3,2,16,1024]{4,3,2,1,0:T(8,128)(2,1)S(1)}, u32[]{:S(2)}, u32[]{:S(2)}) %collective-permute-start) | collective-permute-done | bytes 1572896 | tf_op jit(solution)/shard_map/ppermute | solution.py:14
  80.4 0.0 collective-permute-done.1
  80.4 1.9 pad_maximum_fusion
  82.3 0.0 all-gather.2.cloned.1.call-update
  82.3 0.0 all-reduce.6.cloned.1.call-start
  82.4 0.0 copy-done.5
  82.4 0.1 reshape.52
  82.5 0.0 copy-done.2
  82.5 84.3 %all-gather.2.cloned.1.call-done = bf16[32,3,4,16,1024]{4,3,2,1,0:T(8,128)(2,1)} async-done(((bf16[8,3,4,16,1024]{4,3,2,1,0:T(8,128)(2,1)}), bf16[32,3,4,16,1024]{4,3,2,1,0:T(8,128)(2,1)}) %all-gather.2.cloned.1.call-update) | async-done | bytes 12582928 | tf_op jit(solution)/shard_map/all_gather | solution.py:84
  166.8 5.6 %fusion.29 = (bf16[32,3,2,16,1024]{4,3,2,1,0:T(8,128)(2,1)S(1)}, bf16[32,3,2,16,1024]{4,3,2,1,0:T(8,128)(2,1)S(1)}) fusion(bf16[32,3,4,16,1024]{4,3,2,1,0:T(8,128)(2,1)} %all-gather.2.cloned.1.call-done), kind=kLoop, calls=%fused_computation.63 | loop fusion | bytes 25165824 | tf_op jit(solution)/shard_map/slice | solution.py:85
  172.3 14.7 %maximum_convert_fusion = f32[2,16,3,6,16,1024]{5,4,3,2,1,0:T(8,128)} fusion(bf16[2,16,3,2,16,1024]{5,4,3,2,1,0:T(8,128)(2,1)S(1)} %bitcast.54, bf16[2,16,3,2,16,1024]{5,4,3,2,1,0:T(8,128)(2,1)} %param.9, bf16[2,16,3,2,16,1024]{5,4,3,2,1,0:T(8,128)(2,1)S(1)} %bitcast.53), kind=kLoop, calls=%fused_computation.19 | loop fusion | flops 28311552 | bytes 56623104 | tf_op jit(solution)/shard_map/convert_element_type | solution.py:87
  187.0 31.9 %fusion.14 = (f32[2,16,3,2,16,1024]{5,4,3,2,1,0:T(8,128)}, f32[2,16,3,2,16,1024]{5,4,3,2,1,0:T(8,128)}) fusion(f32[2,16,3,6,16,1024]{5,4,3,2,1,0:T(8,128)} %maximum_convert_fusion), kind=kLoop, calls=%fused_computation.36 | loop fusion | flops 15728640 | bytes 88080384 | tf_op jit(solution)/shard_map/div | solution.py:37
  218.9 43.1 %fusion.11 = (f32[2,16,3,2,16,1024]{5,4,3,2,1,0:T(8,128)}, f32[2,16,3,2,16,1024]{5,4,3,2,1,0:T(8,128)}) fusion(f32[2,16,3,2,16,1024]{5,4,3,2,1,0:T(8,128)} %get-tuple-element.231), kind=kLoop, calls=%fused_computation.32 | loop fusion | flops 31457280 | bytes 37748736 | tf_op jit(solution)/shard_map/div | solution.py:29
  262.0 0.0 copy-done.3
  262.0 6.4 %fusion.22 = (bf16[2,16,6,2,16,1024]{5,4,3,2,1,0:T(8,128)(2,1)S(1)}, f32[2,16,1,2,16,1024]{5,4,3,2,1,0:T(8,128)S(1)}) fusion(f32[2,16,3,2,16,1024]{5,4,3,2,1,0:T(8,128)} %get-tuple-element.233, f32[2,16,1024]{2,1,0:T(8,128)S(1)} %broadcast_multiply_fusion, f32[2,16,3,2,16,1024]{5,4,3,2,1,0:T(8,128)} %get-tuple-element.230, ...), kind=kLoop, calls=%fused_computation.53 | loop fusion | flops 6291455 | bytes 19136512
  268.4 0.0 slice-start
  268.4 3.5 fusion.23
  271.9 0.0 slice-start.1
  271.9 3.5 fusion.24
  275.3 0.0 slice-start.2
  275.4 4.7 fusion.25
  280.1 0.0 slice-done
  280.1 0.0 slice-done.1
  280.1 0.0 slice-done.2
  280.1 0.0 copy-start.4
  280.1 3.3 fusion.26
  283.5 3.3 fusion.27
  286.8 0.0 copy-start
  286.8 4.5 copy-done
  291.3 0.0 copy-done.4
  291.3 162.3 %while.16 = (s32[]{:T(128)}, f32[2,2,16,1024]{3,2,1,0:T(8,128)S(1)}, s32[4]{0:T(128)S(1)}, f32[2,2,9]{2,1,0:T(2,128)}, bf16[2,16,6,2,16,1024]{5,4,3,2,1,0:T(8,12...) while((s32[]{:T(128)}, ...), condition=%wide.region_2.3_spmd.clone, body=%wide.region_0.2_spmd.sunk.clone.sunk | while | flops 94404624 | bytes 25690652 | solution.py:111
  291.3 6.8 %dynamic-slice_bitcast_fusion.2 = bf16[16,6,2,16,1024]{4,3,2,1,0:T(8,128)(2,1)} fusion(bf16[2,16,6,2,16,1024]{5,4,3,2,1,0:T(8,128)(2,1)} %get-tuple-element.317, s32[]{:T(128)S(6)} %select_n.84), kind=kLoop, calls=%fused_computation.11.clone.1 | loop fusion | bytes 12582916 | tf_op jit(solution)/shard_map/while/body/eval_jaxpr/jit(dynamic_index_in_dim)/squeeze | solution.py:101
  298.1 0.7 constant_dynamic-slice_fusion.4
  298.8 0.7 fusion.33
  299.4 31.1 %fusion.34 = f32[2,16,1024]{2,1,0:T(8,128)S(1)} fusion(bf16[16,6,2,16,1024]{4,3,2,1,0:T(8,128)(2,1)} %dynamic-slice_bitcast_fusion.2, f32[6]{0:T(128)S(1)} %get-tuple-element.323, bf16[2,16,6,2,16,1024]{5,4,3,2,1,0:T(8,128)(2,1)} %get-tuple-element.318, s32[]{:T(128)S(6)} %select_n.86, f32[]{:T(128)} %bitcast.41, f32[]{:T(128)} %bitcast.42, ...), kind=kLoop, calls=%fused_computation.10.clone.1 | loop fusion | flops 94339072 | bytes 12714048 | tf_op jit(solution)/shard_map/while/body/eval_jaxpr/reduce_sum | solution.py:72
  330.6 0.6 dynamic_slice.80
  331.8 6.8 %dynamic-slice_bitcast_fusion.2 = bf16[16,6,2,16,1024]{4,3,2,1,0:T(8,128)(2,1)} fusion(bf16[2,16,6,2,16,1024]{5,4,3,2,1,0:T(8,128)(2,1)} %get-tuple-element.317, s32[]{:T(128)S(6)} %select_n.84), kind=kLoop, calls=%fused_computation.11.clone.1 | loop fusion | bytes 12582916 | tf_op jit(solution)/shard_map/while/body/eval_jaxpr/jit(dynamic_index_in_dim)/squeeze | solution.py:101
  338.6 0.7 constant_dynamic-slice_fusion.4
  339.3 0.7 fusion.33
  340.0 31.2 %fusion.34 = f32[2,16,1024]{2,1,0:T(8,128)S(1)} fusion(bf16[16,6,2,16,1024]{4,3,2,1,0:T(8,128)(2,1)} %dynamic-slice_bitcast_fusion.2, f32[6]{0:T(128)S(1)} %get-tuple-element.323, bf16[2,16,6,2,16,1024]{5,4,3,2,1,0:T(8,128)(2,1)} %get-tuple-element.318, s32[]{:T(128)S(6)} %select_n.86, f32[]{:T(128)} %bitcast.41, f32[]{:T(128)} %bitcast.42, ...), kind=kLoop, calls=%fused_computation.10.clone.1 | loop fusion | flops 94339072 | bytes 12714048 | tf_op jit(solution)/shard_map/while/body/eval_jaxpr/reduce_sum | solution.py:72
  371.2 0.6 dynamic_slice.80
  372.5 6.8 %dynamic-slice_bitcast_fusion.2 = bf16[16,6,2,16,1024]{4,3,2,1,0:T(8,128)(2,1)} fusion(bf16[2,16,6,2,16,1024]{5,4,3,2,1,0:T(8,128)(2,1)} %get-tuple-element.317, s32[]{:T(128)S(6)} %select_n.84), kind=kLoop, calls=%fused_computation.11.clone.1 | loop fusion | bytes 12582916 | tf_op jit(solution)/shard_map/while/body/eval_jaxpr/jit(dynamic_index_in_dim)/squeeze | solution.py:101
  379.2 0.7 constant_dynamic-slice_fusion.4
  379.9 0.7 fusion.33
  380.6 31.1 %fusion.34 = f32[2,16,1024]{2,1,0:T(8,128)S(1)} fusion(bf16[16,6,2,16,1024]{4,3,2,1,0:T(8,128)(2,1)} %dynamic-slice_bitcast_fusion.2, f32[6]{0:T(128)S(1)} %get-tuple-element.323, bf16[2,16,6,2,16,1024]{5,4,3,2,1,0:T(8,128)(2,1)} %get-tuple-element.318, s32[]{:T(128)S(6)} %select_n.86, f32[]{:T(128)} %bitcast.41, f32[]{:T(128)} %bitcast.42, ...), kind=kLoop, calls=%fused_computation.10.clone.1 | loop fusion | flops 94339072 | bytes 12714048 | tf_op jit(solution)/shard_map/while/body/eval_jaxpr/reduce_sum | solution.py:72
  411.7 0.6 dynamic_slice.80
  413.0 6.8 %dynamic-slice_bitcast_fusion.2 = bf16[16,6,2,16,1024]{4,3,2,1,0:T(8,128)(2,1)} fusion(bf16[2,16,6,2,16,1024]{5,4,3,2,1,0:T(8,128)(2,1)} %get-tuple-element.317, s32[]{:T(128)S(6)} %select_n.84), kind=kLoop, calls=%fused_computation.11.clone.1 | loop fusion | bytes 12582916 | tf_op jit(solution)/shard_map/while/body/eval_jaxpr/jit(dynamic_index_in_dim)/squeeze | solution.py:101
  419.8 0.7 constant_dynamic-slice_fusion.4
  420.4 0.7 fusion.33
  421.1 31.2 %fusion.34 = f32[2,16,1024]{2,1,0:T(8,128)S(1)} fusion(bf16[16,6,2,16,1024]{4,3,2,1,0:T(8,128)(2,1)} %dynamic-slice_bitcast_fusion.2, f32[6]{0:T(128)S(1)} %get-tuple-element.323, bf16[2,16,6,2,16,1024]{5,4,3,2,1,0:T(8,128)(2,1)} %get-tuple-element.318, s32[]{:T(128)S(6)} %select_n.86, f32[]{:T(128)} %bitcast.41, f32[]{:T(128)} %bitcast.42, ...), kind=kLoop, calls=%fused_computation.10.clone.1 | loop fusion | flops 94339072 | bytes 12714048 | tf_op jit(solution)/shard_map/while/body/eval_jaxpr/reduce_sum | solution.py:72
  452.3 0.6 dynamic_slice.80
  453.6 0.0 copy-start.1
  453.6 0.7 copy-done.1
  454.3 0.0 all-reduce.6.cloned.1.call-update
  454.3 0.0 copy-done.6
  454.3 0.6 dynamic-slice
  455.5 31.2 %all-reduce.6.cloned.1.call-done = f32[2,2,16,1024]{3,2,1,0:T(8,128)} async-done(((f32[2,2,16,1024]{3,2,1,0:T(8,128)}), f32[2,2,16,1024]{3,2,1,0:T(8,128)}) %all-reduce.6.cloned.1.call-update) | async-done | bytes 262160
  486.7 1.5 constant_dynamic-slice_fusion.1
  (9 shorter events, 0.1 us)
Async XLA Ops:
  6.5 75.8 %copy-start.5 = (s32[2,2]{1,0:T(2,128)S(1)}, s32[2,2]{1,0:T(2,128)}, u32[]{:S(2)}) copy-start(s32[2,2]{1,0:T(2,128)} %param.14) | copy-start | bytes 52
  6.5 75.9 %copy-start.2 = (f32[2,16,1024]{2,1,0:T(8,128)S(1)}, f32[2,16,1024]{2,1,0:T(8,128)}, u32[]{:S(2)}) copy-start(f32[2,16,1024]{2,1,0:T(8,128)} %param.12) | copy-start | bytes 393220
  6.5 160.2 %all-gather.2.cloned.1.call-start = ((), (), s32[]{:S(2)}) async-start(), calls=%async_computation | async-start | bytes 15728640 | tf_op jit(solution)/shard_map/all_gather | solution.py:84
  8.2 72.2 %collective-permute-start = (bf16[8,3,2,16,1024]{4,3,2,1,0:T(8,128)(2,1)S(1)}, bf16[8,3,2,16,1024]{4,3,2,1,0:T(8,128)(2,1)S(1)}, u32[]{:S(2)}, u32[]{:S(2)}) collective-permute-start(bf16[8,3,2,16,1024]{4,3,2,1,0:T(8,128)(2,1)S(1)} %constant_dynamic-slice_fusion.2), channel_id=1, source_target_pairs={{0,1},{1,2},{2,3},{3,4},{4,5},{5,6},{6,7},{8,9},{9,10},{10,11},{11... | collective-permute-start | bytes 4718600 | tf_op jit(solution)/shard_map/ppermute | solution.py:14
  13.1 67.2 %collective-permute-start.1 = (bf16[8,3,2,16,1024]{4,3,2,1,0:T(8,128)(2,1)S(1)}, bf16[8,3,2,16,1024]{4,3,2,1,0:T(8,128)(2,1)S(1)}, u32[]{:S(2)}, u32[]{:S(2)}) collective-permute-start(bf16[8,3,2,16,1024]{4,3,2,1,0:T(8,128)(2,1)S(1)} %constant_dynamic-slice_fusion.2), channel_id=1, source_target_pairs={{1,0},{2,1},{3,2},{4,3},{5,4},{6,5},{7,6},{9,8},{10,9},{11,10},{12... | collective-permute-start | bytes 4718600 | tf_op jit(solution)/shard_map/ppermute | solution.py:15
  82.3 404.4 %all-reduce.6.cloned.1.call-start = ((), (), s32[]{:S(2)}) async-start(), calls=%async_computation.1 | async-start | bytes 524288
  218.9 43.1 %copy-start.3 = (f32[2,16,1024]{2,1,0:T(8,128)S(1)}, f32[2,16,1024]{2,1,0:T(8,128)}, u32[]{:S(2)}) copy-start(f32[2,16,1024]{2,1,0:T(8,128)} %param.11) | copy-start | bytes 393220
  268.4 11.7 %slice-start = ((s8[12582912]{0:T(1024)(128)(4,1)}), s8[4194304]{0:T(1024)(128)(4,1)S(1)}, s32[]{:S(2)}) async-start(s8[12582912]{0:T(1024)(128)(4,1)} %bitcast.51), calls=%async_computation.2 | async-start | bytes 8388608
  271.9 8.2 %slice-start.1 = ((s8[12582912]{0:T(1024)(128)(4,1)}), s8[4194304]{0:T(1024)(128)(4,1)S(1)}, s32[]{:S(2)}) async-start(s8[12582912]{0:T(1024)(128)(4,1)} %bitcast.51), calls=%async_computation.3 | async-start | bytes 8388608
  275.3 4.8 slice-start.2
  280.1 11.2 %copy-start.4 = (f32[6]{0:T(128)S(1)}, f32[6]{0:T(128)}, u32[]{:S(2)}) copy-start(f32[6]{0:T(128)} %constant.131.clone..sunk.2) | copy-start | bytes 76
  286.8 4.5 copy-start
  291.3 163.0 %copy-start.6 = (u32[32]{0:T(128)S(1)}, u32[32]{0:T(128)}, u32[]{:S(2)}) copy-start(u32[32]{0:T(128)} %constant.146) | copy-start | bytes 388
  453.6 0.7 copy-start.1
Sparse Core Ops, SparseCore 0:
  82.4 84.2 all-gather.1
  454.4 32.2 all-reduce.5
where the time goes:
time: 496 us; the launch traced here: 495 us
  other arithmetic  241 us (49%)
  waiting for transfers between devices  181 us (36%)
  local copies, waits for them, and re-layouts  49.5 us (10%)
  between operations  14.2 us (3%)
  starting transfers between devices  6.31 us (1%)
    reduce_sum x4, other arithmetic, contribution(): jnp.sum(filtered * green_one.astype(jnp.float32) * weights, axis=(0, 1))  125 us
    all_gather x1, waiting for transfers between devices, on_device(): every_edge = lax.all_gather(edges, 'rcv', axis=0, tiled=True)  84.3 us
    ppermute x1, waiting for transfers between devices, padded_2(): before = lax.ppermute(last, axis, up)  65.9 us
    div x1, other arithmetic, derivative(): return (8.0 * (window(1) - window(-1)) - (window(2) - window(-2))) / 12.0  43.1 us
    div x1, other arithmetic, depth_derivative(): return (8.0 * (window(1) - window(-1)) - (window(2) - window(-2))) / 12.0  31.9 us
    unnamed x3, waiting for transfers between devices  31.2 us
    squeeze x4, local copies, waits for them, and re-layouts, add_slot(): stress_one = lax.dynamic_index_in_dim(stress, source, 0, keepdims=False)  27.1 us
    unnamed x6, other arithmetic  21.3 us
  transfers between devices with their start and end apart: 4, of which 3 were waited for; matrix products, arithmetic and copies ran while one was open for 0% of the time, Pallas kernels for 0%

commit v1 on v0

--- a/solution.py
+++ b/solution.py
@@ -81,7 +81,13 @@
     mine = lax.dynamic_slice_in_dim(flat, member * share, share, 0)
     grown = padded_2(mine, (("slab", 2),), 2)
     edges = jnp.concatenate([grown[:, :, 0:2], grown[:, :, planes + 2 : planes + 4]], axis=2)
-    every_edge = lax.all_gather(edges, "rcv", axis=0, tiled=True)
+    size = lax.axis_size("rcv")
+    held, blocks = (edges, [edges])
+    for _ in range(size - 1):
+        held = lax.ppermute(held, "rcv", [(i_2, (i_2 + 1) % size) for i_2 in range(size)])
+        blocks.insert(0, held)
+    merged = jnp.concatenate(blocks, axis=0)
+    every_edge = jnp.roll(merged, (lax.axis_index("rcv") + 1) * edges.shape[0], axis=0)
     joined = jnp.concatenate([every_edge[:, :, 0:2], flat, every_edge[:, :, 2:4]], axis=2)
     extended = joined.reshape((sources, snap_count, components, planes + 4, row_count, col_count))
     field = extended.astype(jnp.float32)

time: 496 us -> 563 us (1.14)
  local copies, waits for them, and re-layouts: 49.5 us -> 84.7 us
  waiting for transfers between devices: 181 us -> 208 us
    ppermute x0 -> x3, waiting for transfers between devices: none -> 109 us  [on_device(): lax.ppermute(held, 'rcv', [(i_2, (i_2 + 1) % size) for i_2 in range(size)])]
    all_gather x1 -> x0, waiting for transfers between devices: 84.3 us -> none  [on_device(): every_edge = lax.all_gather(edges, 'rcv', axis=0, tiled=True)]
    unnamed x22 -> x33, local copies, waits for them, and re-layouts: 7.35 us -> 33.9 us
    slice x1, local copies, waits for them, and re-layouts: 5.56 us -> 12.1 us  [on_device(): every_edge[:, :, 0:2]]
    unnamed x3 -> x2, waiting for transfers between devices: 31.2 us -> 33.4 us
  transfers between devices with their start and end apart: 4 -> 6, of which waited for: 3 -> 5; matrix products, arithmetic and copies ran while one was open for 0% -> 0% of each run, Pallas kernels for 0% -> 0%
where the time goes in v1:
time: 563 us; the launch traced here: 562 us
  other arithmetic  246 us (44%)
  waiting for transfers between devices  208 us (37%)
  local copies, waits for them, and re-layouts  84.7 us (15%)
  between operations  14.2 us (3%)
  starting transfers between devices  6.33 us (1%)
    reduce_sum x4, other arithmetic, contribution(): jnp.sum(filtered * green_one.astype(jnp.float32) * weights, axis=(0, 1))  124 us
    ppermute x3, waiting for transfers between devices, on_device(): lax.ppermute(held, 'rcv', [(i_2, (i_2 + 1) % size) for i_2 in range(size)])  109 us
    ppermute x1, waiting for transfers between devices, padded_2(): before = lax.ppermute(last, axis, up)  65.9 us
    div x1, other arithmetic, derivative(): return (8.0 * (window(1) - window(-1)) - (window(2) - window(-2))) / 12.0  43.4 us
    unnamed x33, local copies, waits for them, and re-layouts  33.9 us
    unnamed x2, waiting for transfers between devices  33.4 us
    div x1, other arithmetic, depth_derivative(): return (8.0 * (window(1) - window(-1)) - (window(2) - window(-2))) / 12.0  31.9 us
    squeeze x4, local copies, waits for them, and re-layouts, add_slot(): stress_one = lax.dynamic_index_in_dim(stress, source, 0, keepdims=False)  27.1 us
  transfers between devices with their start and end apart: 6, of which 5 were waited for; matrix products, arithmetic and copies ran while one was open for 0% of the time, Pallas kernels for 0%

profile of v1, /device:TPU:0, one launch (start us, length us, event | category | flops | bytes accessed | tf_op | source)
XLA Modules:
  0.0 561.8 jit_solution(17714681269376043942)
XLA Ops:
  6.5 1.6 constant_dynamic-slice_fusion.3
  8.1 5.0 collective-permute-start
  13.1 1.3 collective-permute-start.1
  14.4 65.9 %collective-permute-done = bf16[8,3,2,16,1024]{4,3,2,1,0:T(8,128)(2,1)S(1)} collective-permute-done((bf16[8,3,2,16,1024]{4,3,2,1,0:T(8,128)(2,1)S(1)}, bf16[8,3,2,16,1024]{4,3,2,1,0:T(8,128)(2,1)S(1)}, u32[]{:S(2)}, u32[]{:S(2)}) %collective-permute-start) | collective-permute-done | bytes 1572896 | tf_op jit(solution)/shard_map/ppermute | solution.py:14
  80.3 0.0 collective-permute-done.1
  80.3 0.3 pad_maximum_fusion
  80.6 0.1 collective-permute-start.2
  80.7 36.7 %collective-permute-done.2 = bf16[8,3,4,16,1024]{4,3,2,1,0:T(8,128)(2,1)S(1)} collective-permute-done((bf16[8,3,4,16,1024]{4,3,2,1,0:T(8,128)(2,1)S(1)}, bf16[8,3,4,16,1024]{4,3,2,1,0:T(8,128)(2,1)S(1)}, u32[]{:S(2)}, u32[]{:S(2)}) %collective-permute-start.2) | collective-permute-done | bytes 3145760 | tf_op jit(solution)/shard_map/ppermute | solution.py:87
  117.4 1.6 copy-done.1
  119.0 0.0 collective-permute-start.3
  119.0 36.8 %collective-permute-done.3 = bf16[8,3,4,16,1024]{4,3,2,1,0:T(8,128)(2,1)} collective-permute-done((bf16[8,3,4,16,1024]{4,3,2,1,0:T(8,128)(2,1)S(1)}, bf16[8,3,4,16,1024]{4,3,2,1,0:T(8,128)(2,1)}, u32[]{:S(2)}, u32[]{:S(2)}) %collective-permute-start.3) | collective-permute-done | bytes 3145760 | tf_op jit(solution)/shard_map/ppermute | solution.py:87
  155.8 0.8 reshape.52
  156.6 1.1 broadcast_multiply_fusion
  157.6 35.2 %collective-permute-done.4 = bf16[8,3,4,16,1024]{4,3,2,1,0:T(8,128)(2,1)} collective-permute-done((bf16[8,3,4,16,1024]{4,3,2,1,0:T(8,128)(2,1)}, bf16[8,3,4,16,1024]{4,3,2,1,0:T(8,128)(2,1)}, u32[]{:S(2)}, u32[]{:S(2)}) %collective-permute-start.4) | collective-permute-done | bytes 3145760 | tf_op jit(solution)/shard_map/ppermute | solution.py:87
  192.8 4.1 constant_dynamic-update-slice_fusion.9
  196.9 4.1 constant_dynamic-update-slice_fusion.8
  201.1 2.3 constant_dynamic-update-slice_fusion.7
  203.3 1.4 constant_dynamic-update-slice_fusion.6
  204.7 1.3 constant_dynamic-update-slice_fusion.5
  206.0 4.1 constant_dynamic-update-slice_fusion.4
  210.1 4.1 constant_dynamic-update-slice_fusion.3
  214.2 2.3 constant_dynamic-update-slice_fusion.2
  216.5 1.3 constant_dynamic-update-slice_fusion.1
  217.8 1.3 constant_dynamic-update-slice_fusion
  219.1 12.1 %constant_dynamic-slice_fusion.1 = (bf16[32,3,2,16,1024]{4,3,2,1,0:T(8,128)(2,1)}, bf16[32,3,2,16,1024]{4,3,2,1,0:T(8,128)(2,1)}) fusion(bf16[64,3,4,16,1024]{4,3,2,1,0:T(8,128)(2,1)} %constant_dynamic-update-slice_fusion, s32[]{:T(128)S(6)} %select_n.85, s32[]{:T(128)S(6)} %add.263), kind=kLoop, calls=%fused_computation.70 | loop fusion | bytes 25165832 | tf_op jit(solution)/shard_map/slice | solution.py:91
  231.2 20.2 %maximum_convert_fusion = f32[2,16,3,6,16,1024]{5,4,3,2,1,0:T(8,128)} fusion(bf16[2,16,3,2,16,1024]{5,4,3,2,1,0:T(8,128)(2,1)} %bitcast.54, bf16[2,16,3,2,16,1024]{5,4,3,2,1,0:T(8,128)(2,1)} %param.9, bf16[2,16,3,2,16,1024]{5,4,3,2,1,0:T(8,128)(2,1)} %bitcast.53), kind=kLoop, calls=%fused_computation.19 | loop fusion | flops 28311552 | bytes 56623104 | tf_op jit(solution)/shard_map/convert_element_type | solution.py:93
  251.5 31.9 %fusion.14 = (f32[2,16,3,2,16,1024]{5,4,3,2,1,0:T(8,128)}, f32[2,16,3,2,16,1024]{5,4,3,2,1,0:T(8,128)}) fusion(f32[2,16,3,6,16,1024]{5,4,3,2,1,0:T(8,128)} %maximum_convert_fusion), kind=kLoop, calls=%fused_computation.36 | loop fusion | flops 15728640 | bytes 88080384 | tf_op jit(solution)/shard_map/div | solution.py:37
  283.4 43.4 %fusion.11 = (f32[2,16,3,2,16,1024]{5,4,3,2,1,0:T(8,128)}, f32[2,16,3,2,16,1024]{5,4,3,2,1,0:T(8,128)}) fusion(f32[2,16,3,2,16,1024]{5,4,3,2,1,0:T(8,128)} %get-tuple-element.231), kind=kLoop, calls=%fused_computation.32 | loop fusion | flops 31457280 | bytes 37748736 | tf_op jit(solution)/shard_map/div | solution.py:29
  326.8 6.3 %fusion.22 = (bf16[2,16,6,2,16,1024]{5,4,3,2,1,0:T(8,128)(2,1)S(1)}, f32[2,16,1,2,16,1024]{5,4,3,2,1,0:T(8,128)S(1)}) fusion(f32[2,16,3,2,16,1024]{5,4,3,2,1,0:T(8,128)} %get-tuple-element.235, f32[2,16,1024]{2,1,0:T(8,128)S(1)} %broadcast_multiply_fusion, f32[2,16,3,2,16,1024]{5,4,3,2,1,0:T(8,128)} %get-tuple-element.230, ...), kind=kLoop, calls=%fused_computation.53 | loop fusion | flops 6291455 | bytes 19136512
  333.2 0.0 copy-start.4
  333.2 0.0 slice-start
  333.2 3.5 fusion.23
  336.7 3.5 fusion.24
  340.2 4.7 fusion.25
  344.9 0.0 copy-start.6
  345.0 3.3 fusion.26
  348.3 3.3 fusion.27
  351.6 4.5 copy-done
  356.1 161.9 %while.16 = (s32[]{:T(128)}, f32[2,2,16,1024]{3,2,1,0:T(8,128)S(1)}, s32[4]{0:T(128)S(1)}, f32[2,2,9]{2,1,0:T(2,128)}, bf16[2,16,6,2,16,1024]{5,4,3,2,1,0:T(8,12...) while((s32[]{:T(128)}, ...), condition=%wide.region_2.3_spmd.clone, body=%wide.region_0.2_spmd.sunk.clone.sunk | while | flops 94404624 | bytes 25690652 | solution.py:117
  356.1 6.8 %dynamic-slice_bitcast_fusion.2 = bf16[16,6,2,16,1024]{4,3,2,1,0:T(8,128)(2,1)} fusion(bf16[2,16,6,2,16,1024]{5,4,3,2,1,0:T(8,128)(2,1)} %get-tuple-element.317, s32[]{:T(128)S(6)} %select_n.99), kind=kLoop, calls=%fused_computation.11.clone.1 | loop fusion | bytes 12582916 | tf_op jit(solution)/shard_map/while/body/eval_jaxpr/jit(dynamic_index_in_dim)/squeeze | solution.py:107
  362.9 0.7 constant_dynamic-slice_fusion.6
  363.6 0.7 fusion.32
  364.2 31.1 %fusion.33 = f32[2,16,1024]{2,1,0:T(8,128)S(1)} fusion(bf16[16,6,2,16,1024]{4,3,2,1,0:T(8,128)(2,1)} %dynamic-slice_bitcast_fusion.2, f32[6]{0:T(128)S(1)} %get-tuple-element.323, bf16[2,16,6,2,16,1024]{5,4,3,2,1,0:T(8,128)(2,1)} %get-tuple-element.318, s32[]{:T(128)S(6)} %select_n.101, f32[]{:T(128)} %bitcast.41, f32[]{:T(128)} %bitcast.42, ...), kind=kLoop, calls=%fused_computation.10.clone.1 | loop fusion | flops 94339072 | bytes 12714048 | tf_op jit(solution)/shard_map/while/body/eval_jaxpr/reduce_sum | solution.py:72
  395.3 0.6 dynamic_slice.85
  396.6 6.8 %dynamic-slice_bitcast_fusion.2 = bf16[16,6,2,16,1024]{4,3,2,1,0:T(8,128)(2,1)} fusion(bf16[2,16,6,2,16,1024]{5,4,3,2,1,0:T(8,128)(2,1)} %get-tuple-element.317, s32[]{:T(128)S(6)} %select_n.99), kind=kLoop, calls=%fused_computation.11.clone.1 | loop fusion | bytes 12582916 | tf_op jit(solution)/shard_map/while/body/eval_jaxpr/jit(dynamic_index_in_dim)/squeeze | solution.py:107
  403.4 0.7 constant_dynamic-slice_fusion.6
  404.1 0.7 fusion.32
  404.7 31.1 %fusion.33 = f32[2,16,1024]{2,1,0:T(8,128)S(1)} fusion(bf16[16,6,2,16,1024]{4,3,2,1,0:T(8,128)(2,1)} %dynamic-slice_bitcast_fusion.2, f32[6]{0:T(128)S(1)} %get-tuple-element.323, bf16[2,16,6,2,16,1024]{5,4,3,2,1,0:T(8,128)(2,1)} %get-tuple-element.318, s32[]{:T(128)S(6)} %select_n.101, f32[]{:T(128)} %bitcast.41, f32[]{:T(128)} %bitcast.42, ...), kind=kLoop, calls=%fused_computation.10.clone.1 | loop fusion | flops 94339072 | bytes 12714048 | tf_op jit(solution)/shard_map/while/body/eval_jaxpr/reduce_sum | solution.py:72
  435.8 0.6 dynamic_slice.85
  437.1 6.8 %dynamic-slice_bitcast_fusion.2 = bf16[16,6,2,16,1024]{4,3,2,1,0:T(8,128)(2,1)} fusion(bf16[2,16,6,2,16,1024]{5,4,3,2,1,0:T(8,128)(2,1)} %get-tuple-element.317, s32[]{:T(128)S(6)} %select_n.99), kind=kLoop, calls=%fused_computation.11.clone.1 | loop fusion | bytes 12582916 | tf_op jit(solution)/shard_map/while/body/eval_jaxpr/jit(dynamic_index_in_dim)/squeeze | solution.py:107
  443.9 0.7 constant_dynamic-slice_fusion.6
  444.5 0.7 fusion.32
  445.2 31.1 %fusion.33 = f32[2,16,1024]{2,1,0:T(8,128)S(1)} fusion(bf16[16,6,2,16,1024]{4,3,2,1,0:T(8,128)(2,1)} %dynamic-slice_bitcast_fusion.2, f32[6]{0:T(128)S(1)} %get-tuple-element.323, bf16[2,16,6,2,16,1024]{5,4,3,2,1,0:T(8,128)(2,1)} %get-tuple-element.318, s32[]{:T(128)S(6)} %select_n.101, f32[]{:T(128)} %bitcast.41, f32[]{:T(128)} %bitcast.42, ...), kind=kLoop, calls=%fused_computation.10.clone.1 | loop fusion | flops 94339072 | bytes 12714048 | tf_op jit(solution)/shard_map/while/body/eval_jaxpr/reduce_sum | solution.py:72
  476.3 0.6 dynamic_slice.85
  477.6 6.8 %dynamic-slice_bitcast_fusion.2 = bf16[16,6,2,16,1024]{4,3,2,1,0:T(8,128)(2,1)} fusion(bf16[2,16,6,2,16,1024]{5,4,3,2,1,0:T(8,128)(2,1)} %get-tuple-element.317, s32[]{:T(128)S(6)} %select_n.99), kind=kLoop, calls=%fused_computation.11.clone.1 | loop fusion | bytes 12582916 | tf_op jit(solution)/shard_map/while/body/eval_jaxpr/jit(dynamic_index_in_dim)/squeeze | solution.py:107
  484.4 0.7 constant_dynamic-slice_fusion.6
  485.0 0.7 fusion.32
  485.7 31.1 %fusion.33 = f32[2,16,1024]{2,1,0:T(8,128)S(1)} fusion(bf16[16,6,2,16,1024]{4,3,2,1,0:T(8,128)(2,1)} %dynamic-slice_bitcast_fusion.2, f32[6]{0:T(128)S(1)} %get-tuple-element.323, bf16[2,16,6,2,16,1024]{5,4,3,2,1,0:T(8,128)(2,1)} %get-tuple-element.318, s32[]{:T(128)S(6)} %select_n.101, f32[]{:T(128)} %bitcast.41, f32[]{:T(128)} %bitcast.42, ...), kind=kLoop, calls=%fused_computation.10.clone.1 | loop fusion | flops 94339072 | bytes 12714048 | tf_op jit(solution)/shard_map/while/body/eval_jaxpr/reduce_sum | solution.py:72
  516.8 0.6 dynamic_slice.85
  518.1 0.7 copy-done.3
  518.7 0.0 all-reduce.6.cloned.1.call-update
  518.8 0.6 dynamic-slice
  520.0 33.4 %all-reduce.6.cloned.1.call-done = f32[2,2,16,1024]{3,2,1,0:T(8,128)} async-done(((f32[2,2,16,1024]{3,2,1,0:T(8,128)}), f32[2,2,16,1024]{3,2,1,0:T(8,128)}) %all-reduce.6.cloned.1.call-update) | async-done | bytes 262160
  553.4 1.5 constant_dynamic-slice_fusion.4
  (24 shorter events, 0.2 us)
Async XLA Ops:
  6.5 546.9 %all-reduce.6.cloned.1.call-start = ((), (), s32[]{:S(2)}) async-start(), calls=%async_computation | async-start | bytes 524288
  8.1 72.2 %collective-permute-start = (bf16[8,3,2,16,1024]{4,3,2,1,0:T(8,128)(2,1)S(1)}, bf16[8,3,2,16,1024]{4,3,2,1,0:T(8,128)(2,1)S(1)}, u32[]{:S(2)}, u32[]{:S(2)}) collective-permute-start(bf16[8,3,2,16,1024]{4,3,2,1,0:T(8,128)(2,1)S(1)} %constant_dynamic-slice_fusion.3), channel_id=1, source_target_pairs={{0,1},{1,2},{2,3},{3,4},{4,5},{5,6},{6,7},{8,9},{9,10},{10,11},{11... | collective-permute-start | bytes 4718600 | tf_op jit(solution)/shard_map/ppermute | solution.py:14
  13.1 67.2 %collective-permute-start.1 = (bf16[8,3,2,16,1024]{4,3,2,1,0:T(8,128)(2,1)S(1)}, bf16[8,3,2,16,1024]{4,3,2,1,0:T(8,128)(2,1)S(1)}, u32[]{:S(2)}, u32[]{:S(2)}) collective-permute-start(bf16[8,3,2,16,1024]{4,3,2,1,0:T(8,128)(2,1)S(1)} %constant_dynamic-slice_fusion.3), channel_id=1, source_target_pairs={{1,0},{2,1},{3,2},{4,3},{5,4},{6,5},{7,6},{9,8},{10,9},{11,10},{12... | collective-permute-start | bytes 4718600 | tf_op jit(solution)/shard_map/ppermute | solution.py:15
  80.6 36.7 %collective-permute-start.2 = (bf16[8,3,4,16,1024]{4,3,2,1,0:T(8,128)(2,1)S(1)}, bf16[8,3,4,16,1024]{4,3,2,1,0:T(8,128)(2,1)S(1)}, u32[]{:S(2)}, u32[]{:S(2)}) collective-permute-start(bf16[8,3,4,16,1024]{4,3,2,1,0:T(8,128)(2,1)S(1)} %pad_maximum_fusion), channel_id=1, source_target_pairs={{0,8},{8,16},{16,24},{24,0},{1,9},{9,17},{17,25},{25,1},{2,10},{10... | collective-permute-start | bytes 9437192 | tf_op jit(solution)/shard_map/ppermute | solution.py:87
  117.4 1.6 copy-start.1
  119.0 36.8 %collective-permute-start.3 = (bf16[8,3,4,16,1024]{4,3,2,1,0:T(8,128)(2,1)S(1)}, bf16[8,3,4,16,1024]{4,3,2,1,0:T(8,128)(2,1)}, u32[]{:S(2)}, u32[]{:S(2)}) collective-permute-start(bf16[8,3,4,16,1024]{4,3,2,1,0:T(8,128)(2,1)S(1)} %collective-permute-done.2), channel_id=1, source_target_pairs={{0,8},{8,16},{16,24},{24,0},{1,9},{9,17},{17,25},{25,1},{2,10},{10... | collective-permute-start | bytes 9437192 | tf_op jit(solution)/shard_map/ppermute | solution.py:87
  155.8 37.0 %collective-permute-start.4 = (bf16[8,3,4,16,1024]{4,3,2,1,0:T(8,128)(2,1)}, bf16[8,3,4,16,1024]{4,3,2,1,0:T(8,128)(2,1)}, u32[]{:S(2)}, u32[]{:S(2)}) collective-permute-start(bf16[8,3,4,16,1024]{4,3,2,1,0:T(8,128)(2,1)} %collective-permute-done.3), channel_id=1, source_target_pairs={{0,8},{8,16},{16,24},{24,0},{1,9},{9,17},{17,25},{25,1},{2,10},{10... | collective-permute-start | bytes 9437192 | tf_op jit(solution)/shard_map/ppermute | solution.py:87
  156.6 44.5 %copy-start.2 = (bf16[8,3,4,16,1024]{4,3,2,1,0:T(8,128)(2,1)S(1)}, bf16[8,3,4,16,1024]{4,3,2,1,0:T(8,128)(2,1)}, u32[]{:S(2)}) copy-start(bf16[8,3,4,16,1024]{4,3,2,1,0:T(8,128)(2,1)} %copy-done.1) | copy-start | bytes 9437188
  283.4 43.4 %copy-start.5 = (f32[2,16,1024]{2,1,0:T(8,128)S(1)}, f32[2,16,1024]{2,1,0:T(8,128)}, u32[]{:S(2)}) copy-start(f32[2,16,1024]{2,1,0:T(8,128)} %param.11) | copy-start | bytes 393220
  333.2 7.0 %copy-start.4 = (f32[2,16,1024]{2,1,0:T(8,128)S(1)}, f32[2,16,1024]{2,1,0:T(8,128)}, u32[]{:S(2)}) copy-start(f32[2,16,1024]{2,1,0:T(8,128)} %param.12) | copy-start | bytes 393220
  333.2 11.7 %slice-start = ((s8[12582912]{0:T(1024)(128)(4,1)}), s8[4194304]{0:T(1024)(128)(4,1)S(1)}, s32[]{:S(2)}) async-start(s8[12582912]{0:T(1024)(128)(4,1)} %bitcast.51), calls=%async_computation.1 | async-start | bytes 8388608
  336.7 8.3 %slice-start.1 = ((s8[12582912]{0:T(1024)(128)(4,1)}), s8[4194304]{0:T(1024)(128)(4,1)S(1)}, s32[]{:S(2)}) async-start(s8[12582912]{0:T(1024)(128)(4,1)} %bitcast.51), calls=%async_computation.2 | async-start | bytes 8388608
  340.2 4.8 slice-start.2
  344.9 11.2 %copy-start.6 = (f32[6]{0:T(128)S(1)}, f32[6]{0:T(128)}, u32[]{:S(2)}) copy-start(f32[6]{0:T(128)} %constant.153.clone..sunk.2) | copy-start | bytes 76
  351.6 4.5 copy-start
  356.1 162.7 %copy-start.7 = (u32[32]{0:T(128)S(1)}, u32[32]{0:T(128)}, u32[]{:S(2)}) copy-start(u32[32]{0:T(128)} %constant.168) | copy-start | bytes 388
  518.0 0.7 copy-start.3
Sparse Core Ops, SparseCore 0:
  518.9 34.4 all-reduce.5
